TPU v7x, 512 devices: a whole 4x8x8 slice. The times are simulated.
512 devices in a mesh: ctx: 64 (over x, z_lo, y), head: 8 (over z_hi, core).
Axes of the slice: x: 4, y: 8, z: 8 (z_hi: 4, z_lo: 2; z = z_hi * 2 + z_lo), core: 2. Of those that a mesh axis runs over, the one named last changes fastest.
Arguments:
- queries: bfloat16 [16384, 4096], P('ctx', 'head'), may hold values from -12 to 12
- keys: bfloat16 [16384, 4096], P('ctx', 'head'), may hold values from -4 to 4
- values: bfloat16 [16384, 4096], P('ctx', 'head'), may hold values from -6 to 6
- pool_weight: bfloat16 [512, 256], P('ctx'), may hold values from -0.375 to 0.375
- out_weight: bfloat16 [4096, 4096], P('head', 'ctx'), may hold values from -0.09375 to 0.09375
- pattern: int32 [128, 7], replicated, may hold values from 0 to 127, as said below
Outputs:
- mixed: bfloat16 [16384, 4096], P('ctx', 'head')
Inputs may be any that keep to these rules, and one draw needn't show every extreme that they name: `pattern`: the flat butterfly with the blocks of each shard relabelled: entry (i, b) names a key block that agrees with block i in all bits above b and differs from it in bit b. For b < 1 the lower bits are arbitrary. For b >= 1 the bits from 1 to b - 1 equal those of i, and over the 2 query blocks of one aligned group of 2 blocks the lowest 1 bits take each of their 2 values once.
All inputs are finite; a program needn't handle non-finite values.
Results may differ from a plain program's by a relative error of at most 0.019.
Values may be sent and summed in bfloat16 or wider, within the bound.
No kernel may reach another device: no remote copies, remote signals or barrier semaphores. Data moves between devices by JAX's collectives and lax.ppermute only.
A program may use at most 64 MiB of HBM per device.

v0:
```python
import jax
import jax.numpy as jnp
from jax import lax
from jax.sharding import PartitionSpec as P

HEAD_DIMENSION = 128
BLK = 128


def partner_2(x, axis, stride):
    return lax.ppermute(x, axis, [(i, i ^ 1 << stride) for i in range(lax.axis_size(axis))])


def merge_scores(running, scores, value_set, einsum_form):
    old_max, row_sum, weighted = running
    row_max = jnp.maximum(old_max, jnp.max(scores, axis=-1))
    weights = jnp.exp(scores - row_max[..., None])
    rescale = jnp.exp(old_max - row_max)
    row_sum = row_sum * rescale + jnp.sum(weights, axis=-1)
    weighted = weighted * rescale[..., None] + jnp.einsum(
        einsum_form, weights.astype(jnp.bfloat16), value_set, preferred_element_type=jnp.float32
    )
    return (row_max, row_sum, weighted)


def on_device(queries, keys, values, pool_weight, out_weight, pattern):
    tok_rows, col_width = queries.shape
    local_heads = col_width // HEAD_DIMENSION
    block_count = tok_rows // BLK
    local_bits = block_count.bit_length() - 1
    remote_bits = lax.axis_size("ctx").bit_length() - 1
    score_scale = HEAD_DIMENSION ** (-0.5)
    own_index = lax.axis_index("ctx")
    own_rows = lax.dynamic_slice_in_dim(pattern, own_index * block_count, block_count, 0)
    query_blk = queries.reshape(block_count, BLK, local_heads, HEAD_DIMENSION)
    key_rows = keys.reshape(block_count, BLK, col_width)
    value_rows = values.reshape(block_count, BLK, col_width)
    running = (
        jnp.full((block_count, local_heads, BLK), -jnp.inf, jnp.float32),
        jnp.zeros((block_count, local_heads, BLK), jnp.float32),
        jnp.zeros((block_count, local_heads, BLK, HEAD_DIMENSION), jnp.float32),
    )
    near_index = jnp.concatenate(
        [
            jnp.arange(block_count, dtype=jnp.int32)[:, None],
            own_rows[:, :local_bits] - own_index * block_count,
        ],
        axis=1,
    )
    near_keys = jnp.take(key_rows, near_index, axis=0).reshape(
        block_count, -1, local_heads, HEAD_DIMENSION
    )
    near_values = jnp.take(value_rows, near_index, axis=0).reshape(
        block_count, -1, local_heads, HEAD_DIMENSION
    )
    scores = (
        jnp.einsum("bqhd,bkhd->bhqk", query_blk, near_keys, preferred_element_type=jnp.float32)
        * score_scale
    )
    running = merge_scores(running, scores, near_values, "bhqk,bkhd->bhqd")
    pooled_landmark_keys = jnp.dot(pool_weight, keys, preferred_element_type=jnp.float32).astype(
        jnp.bfloat16
    )
    pooled_landmark_values = jnp.dot(
        pool_weight, values, preferred_element_type=jnp.float32
    ).astype(jnp.bfloat16)
    piece_keys = lax.all_gather(pooled_landmark_keys, "ctx", axis=0, tiled=True).reshape(
        -1, local_heads, HEAD_DIMENSION
    )
    piece_values = lax.all_gather(pooled_landmark_values, "ctx", axis=0, tiled=True).reshape(
        -1, local_heads, HEAD_DIMENSION
    )
    mark_scores = (
        jnp.einsum("bqhd,khd->bhqk", query_blk, piece_keys, preferred_element_type=jnp.float32)
        * score_scale
    )
    running = merge_scores(running, mark_scores, piece_values, "bhqk,khd->bhqd")
    for level in range(remote_bits):
        partner = jnp.bitwise_xor(own_index, 1 << level)
        wanted = own_rows[:, local_bits + level] - partner * block_count
        recv_keys, recv_values = partner_2((key_rows, value_rows), "ctx", level)
        far_keys = jnp.take(recv_keys, wanted, axis=0)
        far_values = jnp.take(recv_values, wanted, axis=0)
        far_scores = (
            jnp.einsum(
                "bqhd,bkhd->bhqk",
                query_blk,
                far_keys.reshape(block_count, BLK, local_heads, HEAD_DIMENSION),
                preferred_element_type=jnp.float32,
            )
            * score_scale
        )
        running = merge_scores(
            running,
            far_scores,
            far_values.reshape(block_count, BLK, local_heads, HEAD_DIMENSION),
            "bhqk,bkhd->bhqd",
        )
    row_max, row_sum, weighted = running
    attended = (
        (weighted / row_sum[..., None])
        .transpose(0, 2, 1, 3)
        .reshape(tok_rows, col_width)
        .astype(jnp.bfloat16)
    )
    partial_value = jnp.dot(
        attended,
        lax.all_gather(out_weight, "ctx", axis=1, tiled=True),
        preferred_element_type=jnp.float32,
    )
    return lax.psum_scatter(
        partial_value.astype(jnp.bfloat16), "head", scatter_dimension=1, tiled=True
    )


def solution(mesh):
    in_specs = (
        P("ctx", "head"),
        P("ctx", "head"),
        P("ctx", "head"),
        P("ctx", None),
        P("head", "ctx"),
        P(),
    )
    out_specs = P("ctx", "head")
    return jax.shard_map(
        on_device, mesh=mesh, in_specs=in_specs, out_specs=out_specs, check_vma=False
    )
```

profile of v0, /device:TPU:28, one launch (start us, length us, event | category | flops | bytes accessed | tf_op | source)
XLA Modules:
  0.0 505.4 jit_solution(15221089490795249946)
XLA Ops:
  6.5 5.2 %collective-permute-start.4 = (bf16[2,128,512]{2,1,0:T(8,128)(2,1)}, bf16[2,128,512]{2,1,0:T(8,128)(2,1)}, u32[]{:S(2)}, u32[]{:S(2)}) collective-permute-start(bf16[2,128,512]{2,1,0:T(8,128)(2,1)} %bitcast.272), channel_id=1, source_target_pairs={{0,32},{8,40},{16,48},{24,56},{32,0},{40,8},{48,16},{56,24},{64,96... | collective-permute-start | bytes 786440 | tf_op jit(solution)/shard_map/ppermute | solution.py:11
  11.7 4.3 collective-permute-start.6
  16.0 4.7 collective-permute-start.5
  22.7 2.4 collective-permute-start
  29.6 137.3 %all_gather.9 = bf16[512,512]{1,0:T(8,128)(2,1)S(1)} all-gather(bf16[8,512]{1,0:T(8,128)(2,1)S(1)} %convolution_convert_fusion.2), channel_id=1, replica_groups=mesh['ctx'=64,'head'=8] {'ctx'}, dimensions={0}, use_global_device_ids=true | all-gather | bytes 532480 | tf_op jit(solution)/shard_map/all_gather | solution.py:67
  170.1 135.2 %all_gather.10 = bf16[512,512]{1,0:T(8,128)(2,1)S(1)} all-gather(bf16[8,512]{1,0:T(8,128)(2,1)S(1)} %convolution_convert_fusion.1), channel_id=1, replica_groups=mesh['ctx'=64,'head'=8] {'ctx'}, dimensions={0}, use_global_device_ids=true | all-gather | bytes 532480 | tf_op jit(solution)/shard_map/all_gather | solution.py:70
  307.9 2.3 collective-permute-start.1
  310.2 2.2 gather_fusion.6
  312.4 6.4 %collective-permute-start.2 = (bf16[2,128,512]{2,1,0:T(8,128)(2,1)}, bf16[2,128,512]{2,1,0:T(8,128)(2,1)}, u32[]{:S(2)}, u32[]{:S(2)}) collective-permute-start(bf16[2,128,512]{2,1,0:T(8,128)(2,1)} %bitcast.276), channel_id=1, source_target_pairs={{0,16},{8,24},{16,0},{24,8},{32,48},{40,56},{48,32},{56,40},{64,80... | collective-permute-start | bytes 786440 | tf_op jit(solution)/shard_map/ppermute | solution.py:11
  318.8 2.2 gather_fusion.7
  323.0 2.2 gather_fusion.8
  325.2 21.4 %collective-permute-start.8 = (bf16[2,128,512]{2,1,0:T(8,128)(2,1)}, bf16[2,128,512]{2,1,0:T(8,128)(2,1)}, u32[]{:S(2)}, u32[]{:S(2)}) collective-permute-start(bf16[2,128,512]{2,1,0:T(8,128)(2,1)} %bitcast.277), channel_id=1, source_target_pairs={{0,128},{8,136},{16,144},{24,152},{32,160},{40,168},{48,176},{56,1... | collective-permute-start | bytes 786440 | tf_op jit(solution)/shard_map/ppermute | solution.py:11
  346.6 2.2 gather_fusion.9
  348.9 2.3 broadcast_select_fusion.6
  356.7 2.2 gather_fusion.2
  358.9 24.6 %collective-permute-start.11 = (bf16[2,128,512]{2,1,0:T(8,128)(2,1)}, bf16[2,128,512]{2,1,0:T(8,128)(2,1)}, u32[]{:S(2)}, u32[]{:S(2)}) collective-permute-start(bf16[2,128,512]{2,1,0:T(8,128)(2,1)} %bitcast.4), channel_id=1, source_target_pairs={{0,256},{8,264},{16,272},{24,280},{32,288},{40,296},{48,304},{56,3... | collective-permute-start | bytes 786440 | tf_op jit(solution)/shard_map/ppermute | solution.py:11
  387.8 2.2 gather_fusion.4
  390.0 2.2 gather_fusion.5
  392.2 2.3 broadcast_select_fusion.10
  402.5 2.2 gather_fusion.13
  404.7 2.2 gather_fusion.12
  407.0 2.3 broadcast_select_fusion.3
  442.1 4.8 convolution_convert_fusion
  447.0 51.6 %reduce-scatter.2.cloned.1.call-done = bf16[256,512]{1,0:T(8,128)(2,1)} async-done(((bf16[256,4096]{1,0:T(8,128)(2,1)}), bf16[256,512]{1,0:T(8,128)(2,1)}) %reduce-scatter.2.cloned.1.call-update) | async-done | bytes 262160 | tf_op jit(solution)/shard_map/reduce_scatter | solution.py:111
  (131 shorter events, 64.4 us)
Async XLA Ops:
  6.5 22.8 %copy-start = (bf16[8,256]{1,0:T(8,128)(2,1)S(1)}, bf16[8,256]{1,0:T(8,128)(2,1)}, u32[]{:S(2)}) copy-start(bf16[8,256]{1,0:T(8,128)(2,1)} %param.13) | copy-start | bytes 12292
  6.5 22.8 %copy-start.7 = (bf16[256,512]{1,0:T(8,128)(2,1)S(1)}, bf16[256,512]{1,0:T(8,128)(2,1)}, u32[]{:S(2)}) copy-start(bf16[256,512]{1,0:T(8,128)(2,1)} %param.11) | copy-start | bytes 786436
  6.5 435.6 %all-gather.2.cloned.1.call-start = ((), (), s32[]{:S(2)}) async-start(), calls=%async_computation.1 | async-start | bytes 4259840 | tf_op jit(solution)/shard_map/all_gather | solution.py:108
  6.5 301.3 %collective-permute-start.4 = (bf16[2,128,512]{2,1,0:T(8,128)(2,1)}, bf16[2,128,512]{2,1,0:T(8,128)(2,1)}, u32[]{:S(2)}, u32[]{:S(2)}) collective-permute-start(bf16[2,128,512]{2,1,0:T(8,128)(2,1)} %bitcast.272), channel_id=1, source_target_pairs={{0,32},{8,40},{16,48},{24,56},{32,0},{40,8},{48,16},{56,24},{64,96... | collective-permute-start | bytes 786440 | tf_op jit(solution)/shard_map/ppermute | solution.py:11
  11.7 309.3 %collective-permute-start.6 = (bf16[2,128,512]{2,1,0:T(8,128)(2,1)}, bf16[2,128,512]{2,1,0:T(8,128)(2,1)}, u32[]{:S(2)}, u32[]{:S(2)}) collective-permute-start(bf16[2,128,512]{2,1,0:T(8,128)(2,1)} %bitcast.273), channel_id=1, source_target_pairs={{0,64},{8,72},{16,80},{24,88},{32,96},{40,104},{48,112},{56,120},{... | collective-permute-start | bytes 786440 | tf_op jit(solution)/shard_map/ppermute | solution.py:11
  16.0 296.4 %collective-permute-start.5 = (bf16[2,128,512]{2,1,0:T(8,128)(2,1)}, bf16[2,128,512]{2,1,0:T(8,128)(2,1)}, u32[]{:S(2)}, u32[]{:S(2)}) collective-permute-start(bf16[2,128,512]{2,1,0:T(8,128)(2,1)} %bitcast.4), channel_id=1, source_target_pairs={{0,32},{8,40},{16,48},{24,56},{32,0},{40,8},{48,16},{56,24},{64,96... | collective-permute-start | bytes 786440 | tf_op jit(solution)/shard_map/ppermute | solution.py:11
  20.7 304.5 %collective-permute-start.7 = (bf16[2,128,512]{2,1,0:T(8,128)(2,1)}, bf16[2,128,512]{2,1,0:T(8,128)(2,1)}, u32[]{:S(2)}, u32[]{:S(2)}) collective-permute-start(bf16[2,128,512]{2,1,0:T(8,128)(2,1)} %bitcast.4), channel_id=1, source_target_pairs={{0,64},{8,72},{16,80},{24,88},{32,96},{40,104},{48,112},{56,120},{... | collective-permute-start | bytes 786440 | tf_op jit(solution)/shard_map/ppermute | solution.py:11
  22.7 332.1 %collective-permute-start = (bf16[2,128,512]{2,1,0:T(8,128)(2,1)}, bf16[2,128,512]{2,1,0:T(8,128)(2,1)}, u32[]{:S(2)}, u32[]{:S(2)}) collective-permute-start(bf16[2,128,512]{2,1,0:T(8,128)(2,1)} %bitcast.274), channel_id=1, source_target_pairs={{0,8},{8,0},{16,24},{24,16},{32,40},{40,32},{48,56},{56,48},{64,72... | collective-permute-start | bytes 786440 | tf_op jit(solution)/shard_map/ppermute | solution.py:11
  25.1 473.5 %reduce-scatter.2.cloned.1.call-start = ((), (), s32[]{:S(2)}) async-start(), calls=%async_computation.2 | async-start | bytes 2359296 | tf_op jit(solution)/shard_map/reduce_scatter | solution.py:111
  27.6 139.3 %copy-start.20 = (bf16[256,512]{1,0:T(8,128)(2,1)S(1)}, bf16[256,512]{1,0:T(8,128)(2,1)}, u32[]{:S(2)}) copy-start(bf16[256,512]{1,0:T(8,128)(2,1)} %param.10) | copy-start | bytes 786436
  307.9 51.0 %collective-permute-start.1 = (bf16[2,128,512]{2,1,0:T(8,128)(2,1)}, bf16[2,128,512]{2,1,0:T(8,128)(2,1)}, u32[]{:S(2)}, u32[]{:S(2)}) collective-permute-start(bf16[2,128,512]{2,1,0:T(8,128)(2,1)} %bitcast.4), channel_id=1, source_target_pairs={{0,8},{8,0},{16,24},{24,16},{32,40},{40,32},{48,56},{56,48},{64,72... | collective-permute-start | bytes 786440 | tf_op jit(solution)/shard_map/ppermute | solution.py:11
  312.4 73.3 %collective-permute-start.2 = (bf16[2,128,512]{2,1,0:T(8,128)(2,1)}, bf16[2,128,512]{2,1,0:T(8,128)(2,1)}, u32[]{:S(2)}, u32[]{:S(2)}) collective-permute-start(bf16[2,128,512]{2,1,0:T(8,128)(2,1)} %bitcast.276), channel_id=1, source_target_pairs={{0,16},{8,24},{16,0},{24,8},{32,48},{40,56},{48,32},{56,40},{64,80... | collective-permute-start | bytes 786440 | tf_op jit(solution)/shard_map/ppermute | solution.py:11
  321.1 69.0 %collective-permute-start.3 = (bf16[2,128,512]{2,1,0:T(8,128)(2,1)}, bf16[2,128,512]{2,1,0:T(8,128)(2,1)}, u32[]{:S(2)}, u32[]{:S(2)}) collective-permute-start(bf16[2,128,512]{2,1,0:T(8,128)(2,1)} %bitcast.4), channel_id=1, source_target_pairs={{0,16},{8,24},{16,0},{24,8},{32,48},{40,56},{48,32},{56,40},{64,80... | collective-permute-start | bytes 786440 | tf_op jit(solution)/shard_map/ppermute | solution.py:11
  325.2 72.9 %collective-permute-start.8 = (bf16[2,128,512]{2,1,0:T(8,128)(2,1)}, bf16[2,128,512]{2,1,0:T(8,128)(2,1)}, u32[]{:S(2)}, u32[]{:S(2)}) collective-permute-start(bf16[2,128,512]{2,1,0:T(8,128)(2,1)} %bitcast.277), channel_id=1, source_target_pairs={{0,128},{8,136},{16,144},{24,152},{32,160},{40,168},{48,176},{56,1... | collective-permute-start | bytes 786440 | tf_op jit(solution)/shard_map/ppermute | solution.py:11
  354.8 45.6 %collective-permute-start.9 = (bf16[2,128,512]{2,1,0:T(8,128)(2,1)}, bf16[2,128,512]{2,1,0:T(8,128)(2,1)}, u32[]{:S(2)}, u32[]{:S(2)}) collective-permute-start(bf16[2,128,512]{2,1,0:T(8,128)(2,1)} %bitcast.4), channel_id=1, source_target_pairs={{0,128},{8,136},{16,144},{24,152},{32,160},{40,168},{48,176},{56,1... | collective-permute-start | bytes 786440 | tf_op jit(solution)/shard_map/ppermute | solution.py:11
  358.9 43.6 %collective-permute-start.11 = (bf16[2,128,512]{2,1,0:T(8,128)(2,1)}, bf16[2,128,512]{2,1,0:T(8,128)(2,1)}, u32[]{:S(2)}, u32[]{:S(2)}) collective-permute-start(bf16[2,128,512]{2,1,0:T(8,128)(2,1)} %bitcast.4), channel_id=1, source_target_pairs={{0,256},{8,264},{16,272},{24,280},{32,288},{40,296},{48,304},{56,3... | collective-permute-start | bytes 786440 | tf_op jit(solution)/shard_map/ppermute | solution.py:11
  385.7 19.1 %collective-permute-start.10 = (bf16[2,128,512]{2,1,0:T(8,128)(2,1)}, bf16[2,128,512]{2,1,0:T(8,128)(2,1)}, u32[]{:S(2)}, u32[]{:S(2)}) collective-permute-start(bf16[2,128,512]{2,1,0:T(8,128)(2,1)} %bitcast.278), channel_id=1, source_target_pairs={{0,256},{8,264},{16,272},{24,280},{32,288},{40,296},{48,304},{56,3... | collective-permute-start | bytes 786440 | tf_op jit(solution)/shard_map/ppermute | solution.py:11
  412.9 4.3 copy-start.17
  412.9 5.4 %copy-start.16 = (bf16[2,128,512]{1,2,0:T(8,128)(2,1)S(1)}, bf16[2,128,512]{1,2,0:T(8,128)(2,1)}, u32[]{:S(2)}) copy-start(bf16[2,128,512]{1,2,0:T(8,128)(2,1)} %copy.203) | copy-start | bytes 786436
  412.9 6.6 %copy-start.19 = (bf16[2,128,512]{1,2,0:T(8,128)(2,1)S(1)}, bf16[2,128,512]{1,2,0:T(8,128)(2,1)}, u32[]{:S(2)}) copy-start(bf16[2,128,512]{1,2,0:T(8,128)(2,1)} %copy.233) | copy-start | bytes 786436
  415.0 5.5 %copy-start.18 = (bf16[2,128,512]{1,2,0:T(8,128)(2,1)S(1)}, bf16[2,128,512]{1,2,0:T(8,128)(2,1)}, u32[]{:S(2)}) copy-start(bf16[2,128,512]{1,2,0:T(8,128)(2,1)} %copy.227) | copy-start | bytes 786436
  431.9 4.7 copy-start.6
  431.9 4.8 copy-start.4
  437.3 1.5 copy-start.12
  (11 other events, 13.0 us)
Sparse Core Ops, SparseCore 0:
  25.2 272.9 all-gather.1
  447.1 51.3 reduce-scatter.1
where the time goes:
time: 507 us; the launch traced here: 505 us
  blocking collectives  273 us (54%)
  starting transfers between devices  79.1 us (16%)
  local copies, waits for them, and re-layouts  55.9 us (11%)
  waiting for transfers between devices  51.6 us (10%)
  matrix products  19.7 us (4%)
  between operations  13.9 us (3%)
  other arithmetic  12.6 us (2%)
    all_gather x1, blocking collectives, on_device(): lax.all_gather(pooled_landmark_keys, 'ctx', axis=0, tiled=True)  137 us
    all_gather x1, blocking collectives, on_device(): lax.all_gather(pooled_landmark_values, 'ctx', axis=0, tiled=True)  135 us
    ppermute x12, starting transfers between devices, partner_2(): lax.ppermute(x, axis, [(i, i ^ 1 << stride) for i in range(lax.axis_size(...  79.1 us
    reduce_scatter x1, waiting for transfers between devices, on_device(): lax.psum_scatter(partial_value.astype(jnp.bfloat16), 'head', scatter_dime...  51.6 us
    gather x6, local copies, waits for them, and re-layouts, on_device(): far_keys = jnp.take(recv_keys, wanted, axis=0)  13.3 us
    gather x6, local copies, waits for them, and re-layouts, on_device(): far_values = jnp.take(recv_values, wanted, axis=0)  13.3 us
    select_n x6, local copies, waits for them, and re-layouts, on_device(): far_keys = jnp.take(recv_keys, wanted, axis=0)  10.7 us
  transfers between devices with their start and end apart: 14, of which 1 were waited for; matrix products, arithmetic and copies ran while one was open for 16% of the time, Pallas kernels for 0%

commit v1 on v0

--- a/solution.py
+++ b/solution.py
@@ -64,9 +64,10 @@
     pooled_landmark_values = jnp.dot(
         pool_weight, values, preferred_element_type=jnp.float32
     ).astype(jnp.bfloat16)
-    piece_keys = lax.all_gather(pooled_landmark_keys, "ctx", axis=0, tiled=True).reshape(
-        -1, local_heads, HEAD_DIMENSION
-    )
+    piece_keys = jnp.concatenate(
+        lax.all_to_all(jnp.stack([pooled_landmark_keys] * lax.axis_size("ctx")), "ctx", 0, 0),
+        axis=0,
+    ).reshape(-1, local_heads, HEAD_DIMENSION)
     piece_values = lax.all_gather(pooled_landmark_values, "ctx", axis=0, tiled=True).reshape(
         -1, local_heads, HEAD_DIMENSION
     )

time: 507 us -> 410 us (0.81)
  the two profiles are of different devices: /device:TPU:28 before, /device:TPU:4 now
where the time goes in v1:
time: 410 us; the launch traced here: 409 us
  blocking collectives  138 us (34%)
  waiting for transfers between devices  120 us (29%)
  starting transfers between devices  71.1 us (17%)
  local copies, waits for them, and re-layouts  41.8 us (10%)
  matrix products  17.5 us (4%)
  between operations  14 us (3%)
  other arithmetic  5.58 us (1%)
    all_gather x1, blocking collectives, on_device(): lax.all_gather(pooled_landmark_values, 'ctx', axis=0, tiled=True)  138 us
    reduce_scatter x1, waiting for transfers between devices, on_device(): lax.psum_scatter(partial_value.astype(jnp.bfloat16), 'head', scatter_dime...  75.9 us
    ppermute x12, starting transfers between devices, partner_2(): lax.ppermute(x, axis, [(i, i ^ 1 << stride) for i in range(lax.axis_size(...  59.6 us
    all_gather x1, waiting for transfers between devices, on_device(): lax.all_gather(out_weight, 'ctx', axis=1, tiled=True)  43.6 us
    all_to_all x1, starting transfers between devices, on_device(): lax.all_to_all(jnp.stack([pooled_landmark_keys] * lax.axis_size('ctx')),...  11.5 us
    gather x6, local copies, waits for them, and re-layouts, on_device(): far_values = jnp.take(recv_values, wanted, axis=0)  10.2 us
    select_n x6, local copies, waits for them, and re-layouts, on_device(): far_values = jnp.take(recv_values, wanted, axis=0)  8.89 us
    gather x6, local copies, waits for them, and re-layouts, on_device(): far_keys = jnp.take(recv_keys, wanted, axis=0)  8.84 us
  transfers between devices with their start and end apart: 15, of which 2 were waited for; matrix products, arithmetic and copies ran while one was open for 15% of the time, Pallas kernels for 0%

profile of v1, /device:TPU:4, one launch (start us, length us, event | category | flops | bytes accessed | tf_op | source)
XLA Modules:
  0.0 408.5 jit_solution(2294172362412639087)
XLA Ops:
  6.5 7.9 %collective-permute-start.4 = (bf16[2,128,512]{2,1,0:T(8,128)(2,1)}, bf16[2,128,512]{2,1,0:T(8,128)(2,1)}, u32[]{:S(2)}, u32[]{:S(2)}) collective-permute-start(bf16[2,128,512]{2,1,0:T(8,128)(2,1)} %bitcast.279), channel_id=1, source_target_pairs={{0,32},{8,40},{16,48},{24,56},{32,0},{40,8},{48,16},{56,24},{64,96... | collective-permute-start | bytes 786440 | tf_op jit(solution)/shard_map/ppermute | solution.py:11
  14.4 4.3 %collective-permute-start.6 = (bf16[2,128,512]{2,1,0:T(8,128)(2,1)}, bf16[2,128,512]{2,1,0:T(8,128)(2,1)S(1)}, u32[]{:S(2)}, u32[]{:S(2)}) collective-permute-start(bf16[2,128,512]{2,1,0:T(8,128)(2,1)} %bitcast.280), channel_id=1, source_target_pairs={{0,64},{8,72},{16,80},{24,88},{32,96},{40,104},{48,112},{56,120},{... | collective-permute-start | bytes 786440 | tf_op jit(solution)/shard_map/ppermute | solution.py:11
  18.7 2.0 collective-permute-start.5
  20.7 1.9 collective-permute-start.7
  22.6 3.5 collective-permute-start
  28.1 11.5 %all-to-all-start = ((bf16[64,8,512]{2,1,0:T(8,128)(2,1)}), bf16[64,8,512]{2,1,0:T(8,128)(2,1)}, u32[]{:S(2)}, u32[]{:S(2)}) async-start(bf16[64,8,512]{2,1,0:T(8,128)(2,1)} %stack.2), calls=%async_computation | async-start | bytes 1048576 | tf_op jit(solution)/shard_map/all_to_all | solution.py:68
  45.0 138.2 %all_gather.6 = bf16[512,512]{1,0:T(8,128)(2,1)S(1)} all-gather(bf16[8,512]{1,0:T(8,128)(2,1)S(1)} %convolution_convert_fusion.1), channel_id=1, replica_groups=mesh['ctx'=64,'head'=8] {'ctx'}, dimensions={0}, use_global_device_ids=true | all-gather | bytes 532480 | tf_op jit(solution)/shard_map/all_gather | solution.py:71
  184.7 2.0 collective-permute-start.1
  186.7 1.9 collective-permute-start.2
  191.9 4.8 %collective-permute-start.3 = (bf16[2,128,512]{2,1,0:T(8,128)(2,1)S(1)}, bf16[2,128,512]{2,1,0:T(8,128)(2,1)}, u32[]{:S(2)}, u32[]{:S(2)}) collective-permute-start(bf16[2,128,512]{2,1,0:T(8,128)(2,1)S(1)} %bitcast.276), channel_id=1, source_target_pairs={{0,16},{8,24},{16,0},{24,8},{32,48},{40,56},{48,32},{56,40},{64,80... | collective-permute-start | bytes 786440 | tf_op jit(solution)/shard_map/ppermute | solution.py:11
  197.3 3.3 collective-permute-start.8
  201.2 2.5 collective-permute-start.9
  203.8 23.3 %collective-permute-start.11 = (bf16[2,128,512]{2,1,0:T(8,128)(2,1)S(1)}, bf16[2,128,512]{2,1,0:T(8,128)(2,1)}, u32[]{:S(2)}, u32[]{:S(2)}) collective-permute-start(bf16[2,128,512]{2,1,0:T(8,128)(2,1)S(1)} %bitcast.278), channel_id=1, source_target_pairs={{0,256},{8,264},{16,272},{24,280},{32,288},{40,296},{48,304},{56,3... | collective-permute-start | bytes 786440 | tf_op jit(solution)/shard_map/ppermute | solution.py:11
  227.1 2.1 collective-permute-start.10
  235.1 2.2 gather_fusion.5
  238.9 2.2 gather_fusion.11
  241.1 2.2 gather_fusion.13
  243.3 2.2 gather_fusion.12
  245.9 2.0 broadcast_select_fusion.10
  266.0 2.1 fusion.84
  268.1 2.0 reshape_reshape.3
  277.4 43.6 %all-gather.2.cloned.1.call-done = bf16[512,4096]{0,1:T(8,128)(2,1)} async-done(((bf16[512,64]{0,1:T(8,128)(2,1)}), bf16[512,4096]{0,1:T(8,128)(2,1)}) %all-gather.2.cloned.1.call-update) | async-done | bytes 4194320 | tf_op jit(solution)/shard_map/all_gather | solution.py:109
  321.0 4.8 %convolution_convert_fusion = bf16[256,4096]{1,0:T(8,128)(2,1)} fusion(bf16[512,4096]{0,1:T(8,128)(2,1)} %all-gather.2.cloned.1.call-done, bf16[32,8,4,128]{3,2,1,0:T(4,128)(2,1)S(1)} %bitcast.296), kind=kOutput, calls=%fused_computation.14 | convolution fusion | flops 1074790400 | bytes 6553600 | tf_op jit(solution)/shard_map/dot_general | solution.py:107
  325.8 75.9 %reduce-scatter.2.cloned.1.call-done = bf16[256,512]{1,0:T(8,128)(2,1)} async-done(((bf16[256,4096]{1,0:T(8,128)(2,1)}), bf16[256,512]{1,0:T(8,128)(2,1)}) %reduce-scatter.2.cloned.1.call-update) | async-done | bytes 262160 | tf_op jit(solution)/shard_map/reduce_scatter | solution.py:112
  (131 shorter events, 46.0 us)
Async XLA Ops:
  6.5 19.6 %copy-start = (bf16[8,256]{1,0:T(8,128)(2,1)S(1)}, bf16[8,256]{1,0:T(8,128)(2,1)}, u32[]{:S(2)}) copy-start(bf16[8,256]{1,0:T(8,128)(2,1)} %param.13) | copy-start | bytes 12292
  6.5 34.8 %copy-start.4 = (bf16[256,512]{1,0:T(8,128)(2,1)S(1)}, bf16[256,512]{1,0:T(8,128)(2,1)}, u32[]{:S(2)}) copy-start(bf16[256,512]{1,0:T(8,128)(2,1)} %param.11) | copy-start | bytes 786436
  6.5 35.4 %copy-start.3 = (bf16[256,512]{1,0:T(8,128)(2,1)S(1)}, bf16[256,512]{1,0:T(8,128)(2,1)}, u32[]{:S(2)}) copy-start(bf16[256,512]{1,0:T(8,128)(2,1)} %param.12) | copy-start | bytes 786436
  6.5 178.1 %collective-permute-start.4 = (bf16[2,128,512]{2,1,0:T(8,128)(2,1)}, bf16[2,128,512]{2,1,0:T(8,128)(2,1)}, u32[]{:S(2)}, u32[]{:S(2)}) collective-permute-start(bf16[2,128,512]{2,1,0:T(8,128)(2,1)} %bitcast.279), channel_id=1, source_target_pairs={{0,32},{8,40},{16,48},{24,56},{32,0},{40,8},{48,16},{56,24},{64,96... | collective-permute-start | bytes 786440 | tf_op jit(solution)/shard_map/ppermute | solution.py:11
  14.4 177.5 %collective-permute-start.6 = (bf16[2,128,512]{2,1,0:T(8,128)(2,1)}, bf16[2,128,512]{2,1,0:T(8,128)(2,1)S(1)}, u32[]{:S(2)}, u32[]{:S(2)}) collective-permute-start(bf16[2,128,512]{2,1,0:T(8,128)(2,1)} %bitcast.280), channel_id=1, source_target_pairs={{0,64},{8,72},{16,80},{24,88},{32,96},{40,104},{48,112},{56,120},{... | collective-permute-start | bytes 786440 | tf_op jit(solution)/shard_map/ppermute | solution.py:11
  18.7 168.0 %collective-permute-start.5 = (bf16[2,128,512]{2,1,0:T(8,128)(2,1)}, bf16[2,128,512]{2,1,0:T(8,128)(2,1)}, u32[]{:S(2)}, u32[]{:S(2)}) collective-permute-start(bf16[2,128,512]{2,1,0:T(8,128)(2,1)} %bitcast.272), channel_id=1, source_target_pairs={{0,32},{8,40},{16,48},{24,56},{32,0},{40,8},{48,16},{56,24},{64,96... | collective-permute-start | bytes 786440 | tf_op jit(solution)/shard_map/ppermute | solution.py:11
  20.7 176.6 %collective-permute-start.7 = (bf16[2,128,512]{2,1,0:T(8,128)(2,1)}, bf16[2,128,512]{2,1,0:T(8,128)(2,1)S(1)}, u32[]{:S(2)}, u32[]{:S(2)}) collective-permute-start(bf16[2,128,512]{2,1,0:T(8,128)(2,1)} %bitcast.273), channel_id=1, source_target_pairs={{0,64},{8,72},{16,80},{24,88},{32,96},{40,104},{48,112},{56,120},{... | collective-permute-start | bytes 786440 | tf_op jit(solution)/shard_map/ppermute | solution.py:11
  22.6 178.5 %collective-permute-start = (bf16[2,128,512]{2,1,0:T(8,128)(2,1)}, bf16[2,128,512]{2,1,0:T(8,128)(2,1)S(1)}, u32[]{:S(2)}, u32[]{:S(2)}) collective-permute-start(bf16[2,128,512]{2,1,0:T(8,128)(2,1)} %bitcast.281), channel_id=1, source_target_pairs={{0,8},{8,0},{16,24},{24,16},{32,40},{40,32},{48,56},{56,48},{64,72... | collective-permute-start | bytes 786440 | tf_op jit(solution)/shard_map/ppermute | solution.py:11
  28.1 240.0 %all-to-all-start = ((bf16[64,8,512]{2,1,0:T(8,128)(2,1)}), bf16[64,8,512]{2,1,0:T(8,128)(2,1)}, u32[]{:S(2)}, u32[]{:S(2)}) async-start(bf16[64,8,512]{2,1,0:T(8,128)(2,1)} %stack.2), calls=%async_computation | async-start | bytes 1048576 | tf_op jit(solution)/shard_map/all_to_all | solution.py:68
  39.5 281.4 %all-gather.2.cloned.1.call-start = ((), (), s32[]{:S(2)}) async-start(), calls=%async_computation.2 | async-start | bytes 4259840 | tf_op jit(solution)/shard_map/all_gather | solution.py:109
  40.3 361.4 %reduce-scatter.2.cloned.1.call-start = ((), (), s32[]{:S(2)}) async-start(), calls=%async_computation.3 | async-start | bytes 2359296 | tf_op jit(solution)/shard_map/reduce_scatter | solution.py:112
  184.7 19.1 %collective-permute-start.1 = (bf16[2,128,512]{2,1,0:T(8,128)(2,1)S(1)}, bf16[2,128,512]{2,1,0:T(8,128)(2,1)}, u32[]{:S(2)}, u32[]{:S(2)}) collective-permute-start(bf16[2,128,512]{2,1,0:T(8,128)(2,1)S(1)} %bitcast.275), channel_id=1, source_target_pairs={{0,8},{8,0},{16,24},{24,16},{32,40},{40,32},{48,56},{56,48},{64,72... | collective-permute-start | bytes 786440 | tf_op jit(solution)/shard_map/ppermute | solution.py:11
  186.7 40.4 %collective-permute-start.2 = (bf16[2,128,512]{2,1,0:T(8,128)(2,1)S(1)}, bf16[2,128,512]{2,1,0:T(8,128)(2,1)}, u32[]{:S(2)}, u32[]{:S(2)}) collective-permute-start(bf16[2,128,512]{2,1,0:T(8,128)(2,1)S(1)} %bitcast.283), channel_id=1, source_target_pairs={{0,16},{8,24},{16,0},{24,8},{32,48},{40,56},{48,32},{56,40},{64,80... | collective-permute-start | bytes 786440 | tf_op jit(solution)/shard_map/ppermute | solution.py:11
  191.9 43.2 %collective-permute-start.3 = (bf16[2,128,512]{2,1,0:T(8,128)(2,1)S(1)}, bf16[2,128,512]{2,1,0:T(8,128)(2,1)}, u32[]{:S(2)}, u32[]{:S(2)}) collective-permute-start(bf16[2,128,512]{2,1,0:T(8,128)(2,1)S(1)} %bitcast.276), channel_id=1, source_target_pairs={{0,16},{8,24},{16,0},{24,8},{32,48},{40,56},{48,32},{56,40},{64,80... | collective-permute-start | bytes 786440 | tf_op jit(solution)/shard_map/ppermute | solution.py:11
  197.3 40.1 %collective-permute-start.8 = (bf16[2,128,512]{2,1,0:T(8,128)(2,1)S(1)}, bf16[2,128,512]{2,1,0:T(8,128)(2,1)}, u32[]{:S(2)}, u32[]{:S(2)}) collective-permute-start(bf16[2,128,512]{2,1,0:T(8,128)(2,1)S(1)} %bitcast.284), channel_id=1, source_target_pairs={{0,128},{8,136},{16,144},{24,152},{32,160},{40,168},{48,176},{56,1... | collective-permute-start | bytes 786440 | tf_op jit(solution)/shard_map/ppermute | solution.py:11
  201.2 28.0 %copy-start.19 = (bf16[2,128,512]{2,1,0:T(8,128)(2,1)}, bf16[2,128,512]{2,1,0:T(8,128)(2,1)S(1)}, u32[]{:S(2)}) copy-start(bf16[2,128,512]{2,1,0:T(8,128)(2,1)S(1)} %collective-permute-done) | copy-start | bytes 786436
  201.2 37.7 %collective-permute-start.9 = (bf16[2,128,512]{2,1,0:T(8,128)(2,1)S(1)}, bf16[2,128,512]{2,1,0:T(8,128)(2,1)}, u32[]{:S(2)}, u32[]{:S(2)}) collective-permute-start(bf16[2,128,512]{2,1,0:T(8,128)(2,1)S(1)} %bitcast.277), channel_id=1, source_target_pairs={{0,128},{8,136},{16,144},{24,152},{32,160},{40,168},{48,176},{56,1... | collective-permute-start | bytes 786440 | tf_op jit(solution)/shard_map/ppermute | solution.py:11
  203.8 37.4 %collective-permute-start.11 = (bf16[2,128,512]{2,1,0:T(8,128)(2,1)S(1)}, bf16[2,128,512]{2,1,0:T(8,128)(2,1)}, u32[]{:S(2)}, u32[]{:S(2)}) collective-permute-start(bf16[2,128,512]{2,1,0:T(8,128)(2,1)S(1)} %bitcast.278), channel_id=1, source_target_pairs={{0,256},{8,264},{16,272},{24,280},{32,288},{40,296},{48,304},{56,3... | collective-permute-start | bytes 786440 | tf_op jit(solution)/shard_map/ppermute | solution.py:11
  227.1 16.2 %collective-permute-start.10 = (bf16[2,128,512]{2,1,0:T(8,128)(2,1)S(1)}, bf16[2,128,512]{2,1,0:T(8,128)(2,1)}, u32[]{:S(2)}, u32[]{:S(2)}) collective-permute-start(bf16[2,128,512]{2,1,0:T(8,128)(2,1)S(1)} %bitcast.285), channel_id=1, source_target_pairs={{0,256},{8,264},{16,272},{24,280},{32,288},{40,296},{48,304},{56,3... | collective-permute-start | bytes 786440 | tf_op jit(solution)/shard_map/ppermute | solution.py:11
  245.5 2.4 copy-start.13
  245.5 2.4 copy-start.14
  245.5 2.4 copy-start.15
  249.0 7.1 %copy-start.17 = (bf16[2,128,512]{2,1,0:T(8,128)(2,1)S(1)}, bf16[2,128,512]{2,1,0:T(8,128)(2,1)}, u32[]{:S(2)}) copy-start(bf16[2,128,512]{2,1,0:T(8,128)(2,1)} %get-tuple-element.82) | copy-start | bytes 786436
  249.0 7.9 %copy-start.16 = (bf16[2,128,512]{2,1,0:T(8,128)(2,1)S(1)}, bf16[2,128,512]{2,1,0:T(8,128)(2,1)}, u32[]{:S(2)}) copy-start(bf16[2,128,512]{2,1,0:T(8,128)(2,1)} %get-tuple-element.57) | copy-start | bytes 786436
  (11 other events, 14.4 us)
Sparse Core Ops, SparseCore 0:
  42.5 278.4 all-gather.1
  325.9 75.7 reduce-scatter.1
